TPU v7x, 32 devices: a whole 2x2x4 slice. The times are simulated.
32 devices in a mesh: seq: 8 (over z, y), head: 4 (over x, core).
Axes of the slice: x: 2, y: 2, z: 4, core: 2. Of those that a mesh axis runs over, the one named last changes fastest.
Arguments:
- hidden_states: bfloat16 [4096, 4096], P('seq', 'head'), may hold values from -64 to 64
- out_grad: bfloat16 [4096, 4096], P('seq', 'head'), may hold values from -96 to 96
- encodings: bfloat16 [4096, 896], P('seq'), may hold values from -9 to 9
- w_query: bfloat16 [4096, 2048], P(None, 'head'), may hold values from -1 to 1
- w_key: bfloat16 [896, 2048], P(None, 'head'), may hold values from -1 to 1
- w_value: bfloat16 [896, 2048], P(None, 'head'), may hold values from -0.1875 to 0.1875
- w_out: bfloat16 [2048, 4096], P('head'), may hold values from -0.125 to 0.125
- neighbour_ids: int32 [64, 2], P('seq'), may hold values from 0 to 31, as said below
- neighbour_counts: int32 [64], P('seq'), may hold values from 1 to 2
Outputs:
- hidden_grad: bfloat16 [4096, 4096], P(('seq', 'head'))
- enc_grad: bfloat16 [4096, 896], P('seq', 'head')
Inputs may be any that keep to these rules, and one draw needn't show every extreme that they name: `neighbour_ids`: record b lies in the shard of seq index b // 4. The 16 entries of the spans of one seq index name at most 2 records of any one shard, and exactly 2 of one shard that every seq index names so.
All inputs are finite; a program needn't handle non-finite values.
Results may differ from a plain program's by a relative error of at most 0.01.
The roundings to bfloat16 on the way count: a program that leaves them out, or rounds other values in their place, can miss the bound.
Values may be sent and summed in bfloat16 or wider, within the bound.
No kernel may reach another device: no remote copies, remote signals or barrier semaphores. Data moves between devices by JAX's collectives and lax.ppermute only.
A program may use at most 128 MiB of HBM per device.

v0:
```python
import math
import jax
import jax.numpy as jnp
from jax import lax
from jax.sharding import PartitionSpec as P

HD = 128
SPAN = 64
NEIGH = 2
RET = 128


def attend_spans(queries, attend_grad, key_rows, value_rows, record_counts):
    row_count = queries.shape[0]
    columns = queries.shape[1]
    heads_here = columns // HD
    spans_here = row_count // SPAN
    shift_by = SPAN - 1
    score_scale = 1.0 / math.sqrt(HD)
    has_keys = jnp.arange(row_count) < row_count - shift_by
    query_rows = jnp.roll(queries, -shift_by, axis=0).reshape(spans_here, SPAN, heads_here, HD)
    grad_rows = jnp.where(
        has_keys[:, None], jnp.roll(attend_grad, -shift_by, axis=0), jnp.zeros((), jnp.bfloat16)
    )
    grad_rows = grad_rows.reshape(spans_here, SPAN, heads_here, HD)
    key_spans = key_rows.reshape(spans_here, NEIGH * RET, heads_here, HD)
    value_spans = value_rows.reshape(spans_here, NEIGH * RET, heads_here, HD)
    in_use = jnp.arange(NEIGH)[None, :] < record_counts[:, None]
    key_in_use = jnp.repeat(in_use, RET, axis=1)
    scores = (
        jnp.einsum("cqhd,ckhd->chqk", query_rows, key_spans, preferred_element_type=jnp.float32)
        * score_scale
    )
    scores = jnp.where(key_in_use[:, None, None, :], scores, -jnp.inf)
    row_top = jnp.max(scores, axis=-1, keepdims=True)
    exponent = jnp.exp(scores - row_top)
    soft_weights = exponent / jnp.sum(exponent, axis=-1, keepdims=True)
    soft_low = soft_weights.astype(jnp.bfloat16)
    outputs = jnp.einsum(
        "chqk,ckhd->cqhd", soft_low, value_spans, preferred_element_type=jnp.float32
    )
    row_delta = jnp.sum(grad_rows.astype(jnp.float32) * outputs, axis=-1)
    prob_grad = jnp.einsum(
        "cqhd,ckhd->chqk", grad_rows, value_spans, preferred_element_type=jnp.float32
    )
    score_grad = soft_weights * (prob_grad - jnp.transpose(row_delta, (0, 2, 1))[..., None])
    score_low = score_grad.astype(jnp.bfloat16)
    query_grad = (
        jnp.einsum("chqk,ckhd->cqhd", score_low, key_spans, preferred_element_type=jnp.float32)
        * score_scale
    ).astype(jnp.bfloat16)
    key_grad = (
        jnp.einsum("chqk,cqhd->ckhd", score_low, query_rows, preferred_element_type=jnp.float32)
        * score_scale
    ).astype(jnp.bfloat16)
    value_grad = jnp.einsum(
        "chqk,cqhd->ckhd", soft_low, grad_rows, preferred_element_type=jnp.float32
    ).astype(jnp.bfloat16)
    query_grad = jnp.roll(query_grad.reshape(row_count, columns), shift_by, axis=0)
    pair_total = spans_here * NEIGH
    return (
        query_grad,
        key_grad.reshape(pair_total, RET, columns),
        value_grad.reshape(pair_total, RET, columns),
    )


def shards(
    hidden_states,
    out_grad,
    encodings,
    w_query,
    w_key,
    w_value,
    w_out,
    neighbour_ids,
    neighbour_counts,
):
    seq_count = lax.axis_size("seq")
    columns = w_query.shape[1]
    record_total = encodings.shape[0] // RET
    requests = neighbour_ids.shape[0] * NEIGH
    slot_cap = max(2, (requests + seq_count - 1) // seq_count)
    slot_total = seq_count * slot_cap
    highest = lax.Precision.HIGHEST
    contract_last = (((1,), (1,)), ((), ()))
    contract_first = (((0,), (0,)), ((), ()))
    hidden_piece = lax.all_gather(hidden_states, "head", axis=1, tiled=True)
    grad_piece = lax.all_gather(out_grad, "head", axis=1, tiled=True)
    query_sum = jnp.dot(hidden_piece, w_query, preferred_element_type=jnp.float32)
    grad_sum = lax.dot_general(grad_piece, w_out, contract_last, preferred_element_type=jnp.float32)
    query_sum, grad_sum = (query_sum, grad_sum)
    queries = query_sum.astype(jnp.bfloat16)
    attend_grad = grad_sum.astype(jnp.bfloat16)
    wanted = neighbour_ids.reshape(requests)
    owner_of = wanted // record_total
    local_record = wanted % record_total
    order_at = jnp.arange(requests)
    earlier_same = (owner_of[:, None] == owner_of[None, :]) & (
        order_at[None, :] < order_at[:, None]
    )
    rank_at = jnp.sum(earlier_same, axis=1)
    slot_at = owner_of * slot_cap + rank_at
    placing = slot_at[:, None] == jnp.arange(slot_total)[None, :]
    placing_low = placing.astype(jnp.bfloat16)
    slot_record = jnp.sum(jnp.where(placing, local_record[:, None], 0), axis=0)
    slot_record = jnp.where(jnp.any(placing, axis=0), slot_record, -1).reshape(seq_count, slot_cap)
    asked = lax.all_to_all(slot_record, "seq", split_axis=0, concat_axis=0, tiled=True).reshape(
        slot_total
    )
    choosing = asked[:, None] == jnp.arange(record_total)[None, :]
    choosing_low = choosing.astype(jnp.bfloat16)
    key_own = jnp.dot(encodings, w_key, preferred_element_type=jnp.float32).astype(jnp.bfloat16)
    value_own = jnp.dot(encodings, w_value, preferred_element_type=jnp.float32).astype(jnp.bfloat16)
    paired_own = jnp.concatenate([key_own, value_own], axis=1).reshape(
        record_total, RET * 2 * columns
    )
    outgoing = jnp.dot(choosing_low, paired_own, preferred_element_type=jnp.float32).astype(
        jnp.bfloat16
    )
    arrived = lax.all_to_all(
        outgoing.reshape(seq_count, slot_cap, RET, 2 * columns),
        "seq",
        split_axis=0,
        concat_axis=0,
        tiled=True,
    )
    fetched = jnp.dot(
        placing_low,
        arrived.reshape(slot_total, RET * 2 * columns),
        preferred_element_type=jnp.float32,
    ).astype(jnp.bfloat16)
    fetched = fetched.reshape(requests, RET, 2 * columns)
    key_rows = fetched[:, :, :columns]
    value_rows = fetched[:, :, columns:]
    query_grad, key_grad, value_grad = attend_spans(
        queries, attend_grad, key_rows, value_rows, neighbour_counts
    )
    paired_grad = jnp.concatenate([key_grad, value_grad], axis=2).reshape(
        requests, RET * 2 * columns
    )
    returning = lax.dot_general(
        placing_low, paired_grad, contract_first, preferred_element_type=jnp.float32
    ).astype(jnp.bfloat16)
    came_back = lax.all_to_all(
        returning.reshape(seq_count, slot_cap, RET, 2 * columns),
        "seq",
        split_axis=0,
        concat_axis=0,
        tiled=True,
    )
    record_grad = lax.dot_general(
        choosing_low,
        came_back.reshape(slot_total, RET * 2 * columns),
        contract_first,
        preferred_element_type=jnp.float32,
    )
    record_grad = record_grad.reshape(record_total * RET, 2 * columns)
    enc_part = lax.dot_general(
        record_grad[:, :columns], w_key.astype(jnp.float32), contract_last, precision=highest
    )
    enc_part = enc_part + lax.dot_general(
        record_grad[:, columns:], w_value.astype(jnp.float32), contract_last, precision=highest
    )
    enc_grad = lax.psum_scatter(enc_part, "head", scatter_dimension=1, tiled=True).astype(
        jnp.bfloat16
    )
    partial_value = lax.dot_general(
        query_grad, w_query, contract_last, preferred_element_type=jnp.float32
    )
    hidden_grad = lax.psum_scatter(
        lax.optimization_barrier(partial_value.astype(jnp.bfloat16))
        .astype(jnp.float32)
        .astype(jnp.bfloat16),
        "head",
        scatter_dimension=0,
        tiled=True,
    )
    return (hidden_grad, enc_grad)


def solution(mesh):
    return jax.shard_map(
        shards,
        mesh=mesh,
        in_specs=(
            P("seq", "head"),
            P("seq", "head"),
            P("seq", None),
            P(None, "head"),
            P(None, "head"),
            P(None, "head"),
            P("head", None),
            P("seq", None),
            P("seq"),
        ),
        out_specs=(P(("seq", "head"), None), P("seq", "head")),
        check_vma=False,
    )
```

profile of v0, /device:TPU:0, one launch (start us, length us, event | category | flops | bytes accessed | tf_op | source)
XLA Modules:
  0.0 382.2 jit_solution(9835484429578831642)
XLA Ops:
  9.8 7.3 %all-to-all-start = ((s32[8,1,2]{2,1,0:T(1,128)}), s32[8,1,2]{2,1,0:T(1,128)S(1)}, u32[]{:S(2)}, u32[]{:S(2)}) async-start(s32[8,1,2]{2,1,0:T(1,128)} %bitcast), calls=%async_computation | async-start | bytes 8192 | tf_op jit(solution)/shard_map/all_to_all | solution.py:108
  17.1 2.4 convolution_convert_fusion.6
  26.1 4.3 %copy.82 = bf16[2,8,128,1024]{3,2,1,0:T(8,128)(2,1)} copy(bf16[2,8,128,1024]{3,1,2,0:T(8,128)(2,1)S(1)} %bitcast.71) | data formatting | bytes 8388608
  30.4 4.7 %all-to-all-start.1 = ((bf16[8,2,128,1024]{3,2,1,0:T(8,128)(2,1)}), bf16[8,2,128,1024]{3,2,1,0:T(8,128)(2,1)}, u32[]{:S(2)}, u32[]{:S(2)}) async-start(bf16[8,2,128,1024]{3,2,1,0:T(8,128)(2,1)} %bitcast.69), calls=%async_computation.1 | async-start | bytes 8388608 | tf_op jit(solution)/shard_map/all_to_all | solution.py:121
  37.7 9.1 %all-gather.5.cloned.1.call-done = bf16[512,4096]{1,0:T(8,128)(2,1)} async-done(((bf16[512,1024]{1,0:T(8,128)(2,1)}), bf16[512,4096]{1,0:T(8,128)(2,1)}) %all-gather.5.cloned.1.call-update) | async-done | bytes 4194320 | tf_op jit(solution)/shard_map/all_gather | solution.py:89
  46.8 5.8 %convolution_convert_fusion.4 = bf16[512,512]{1,0:T(8,128)(2,1)S(1)} fusion(bf16[512,4096]{1,0:T(8,128)(2,1)} %all-gather.5.cloned.1.call-done, bf16[512,4096]{1,0:T(8,128)(2,1)} %param.15), kind=kOutput, calls=%fused_computation.25 | convolution fusion | flops 2147745792 | bytes 8912896 | tf_op jit(solution)/shard_map/dot_general | solution.py:91
  52.7 30.1 %all-gather.3.cloned.1.call-done = bf16[512,4096]{1,0:T(8,128)(2,1)} async-done(((bf16[512,1024]{1,0:T(8,128)(2,1)}), bf16[512,4096]{1,0:T(8,128)(2,1)}) %all-gather.3.cloned.1.call-update) | async-done | bytes 4194320 | tf_op jit(solution)/shard_map/all_gather | solution.py:88
  82.8 5.8 %convolution_convert_fusion.5 = bf16[512,512]{1,0:T(8,128)(2,1)S(1)} fusion(bf16[512,4096]{1,0:T(8,128)(2,1)} %all-gather.3.cloned.1.call-done, bf16[4096,512]{1,0:T(8,128)(2,1)} %param.12), kind=kOutput, calls=%fused_computation.26 | convolution fusion | flops 2147745792 | bytes 8912896 | tf_op jit(solution)/shard_map/dot_general | solution.py:90
  89.9 37.4 %all-to-all-done.1 = bf16[8,2,128,1024]{3,2,1,0:T(8,128)(2,1)} async-done(((bf16[8,2,128,1024]{3,2,1,0:T(8,128)(2,1)}), bf16[8,2,128,1024]{3,2,1,0:T(8,128)(2,1)}, u32[]{:S(2)}, u32[]{:S(2)}) %all-to-all-start.1) | async-done | bytes 4194336 | tf_op jit(solution)/shard_map/all_to_all | solution.py:121
  127.3 4.5 %copy.83 = bf16[2,8,128,1024]{3,1,2,0:T(8,128)(2,1)S(1)} copy(bf16[2,8,128,1024]{3,2,1,0:T(8,128)(2,1)} %bitcast.11) | data formatting | bytes 8388608
  133.1 2.3 copy.84
  137.2 2.2 reshape.200
  139.5 2.5 reshape.199
  143.4 2.0 fusion.60
  145.4 7.4 %convert_bitcast_fusion = bf16[8,256,4,128]{1,3,2,0:T(8,128)(2,1)} fusion(bf16[8,64,4,128]{3,2,1,0:T(4,128)(2,1)} %concatenate.22, pred[8,64]{1,0:T(8,128)(4,1)} %add_compare_fusion, f32[8,4,64]{2,1,0:T(4,128)S(1)} %get-tuple-element.6, f32[8,4,64,256]{3,2,1,0:T(8,128)} %copy-done.3, pred[8,256]{1,0:T(8,128)(4,1)} %broadcast_bitcast_fusion), kind=kOutput, calls=%fused_computation.7 | convolution fusion | flops 138152192 | bytes 4729344 | tf_op jit(solution)/shard_map/chqk,cqhd->ckhd/dot_general | solution.py:56
  152.8 6.3 %fusion.25 = f32[8,64,4]{1,2,0:T(4,128)} fusion(bf16[8,256,4,128]{3,2,1,0:T(4,128)(2,1)S(1)} %copy-done.5, bf16[8,64,4,128]{3,2,1,0:T(4,128)(2,1)} %concatenate.22, pred[8,64]{1,0:T(8,128)(4,1)} %add_compare_fusion, f32[8,4,64]{2,1,0:T(4,128)S(1)} %get-tuple-element.6, f32[8,4,64,256]{3,2,1,0:T(8,128)} %copy-done.3, pred[8,256]{1,0:T(8,128)(4,1)} %broadcast_bitcast_fusion), kind=kOutput, calls=%fused_computation.30 | convolution fusion | flops 137888000 | bytes 4737536 | tf_op jit(solution)/shard_map/chqk,ckhd->cqhd/dot_general | solution.py:39
  159.1 2.8 copy.74
  161.9 2.2 reshape.191
  164.1 3.3 multiply_convert_fusion.1
  169.6 2.2 reshape.190
  171.8 4.5 %fusion.61 = bf16[2,8,128,1024]{2,1,0,3:T(8,128)(2,1)} fusion(bf16[16,128,512]{1,0,2:T(8,128)(2,1)} %reshape.191, bf16[16,128,512]{1,0,2:T(8,128)(2,1)} %reshape.190), kind=kLoop, calls=%fused_computation.81 | loop fusion | flops 2097152 | bytes 8388608
  176.3 7.6 %copy.86 = bf16[2,8,128,1024]{3,1,2,0:T(8,128)(2,1)} copy(bf16[2,8,128,1024]{2,1,0,3:T(8,128)(2,1)} %fusion.61) | data formatting | bytes 8388608
  184.0 3.5 convolution_convert_fusion
  187.5 2.3 copy.87
  189.8 96.8 %all_to_all.16 = bf16[8,2,128,1024]{3,2,1,0:T(8,128)(2,1)S(1)} all-to-all(bf16[8,2,128,1024]{3,2,1,0:T(8,128)(2,1)S(1)} %bitcast.72), channel_id=1, replica_groups=mesh['seq'=8,'head'=4] {'seq'}, dimensions={0} | all-to-all | bytes 8388608 | tf_op jit(solution)/shard_map/all_to_all | solution.py:145
  286.6 2.3 copy.88
  290.1 2.8 reshape.195
  292.9 3.1 fusion.32
  296.0 3.0 convolution_add_fusion
  301.8 4.3 %convolution_convert_fusion.3 = bf16[512,4096]{1,0:T(8,128)(2,1)} fusion(bf16[4096,512]{1,0:T(8,128)(2,1)S(1)} %copy-done.13, bf16[449,512]{1,0:T(8,128)(2,1)S(1)} %slice.51, bf16[63,512]{1,0:T(8,128)(2,1)S(1)} %slice.50), kind=kOutput, calls=%fused_computation.4 | convolution fusion | flops 2150629376 | bytes 8912896 | tf_op jit(solution)/shard_map/dot_general | solution.py:168
  306.2 21.6 %reduce-scatter.5.cloned.1.call-done = f32[512,224]{0,1:T(8,128)} async-done(((f32[512,896]{0,1:T(8,128)}), f32[512,224]{0,1:T(8,128)}) %reduce-scatter.5.cloned.1.call-update) | async-done | bytes 458768 | tf_op jit(solution)/shard_map/reduce_scatter | solution.py:165
  329.5 45.8 %reduce-scatter.3.cloned.1.call-done = bf16[128,4096]{1,0:T(8,128)(2,1)} async-done(((bf16[512,4096]{1,0:T(8,128)(2,1)}), bf16[128,4096]{1,0:T(8,128)(2,1)}) %reduce-scatter.3.cloned.1.call-update) | async-done | bytes 1048592 | tf_op jit(solution)/shard_map/reduce_scatter | solution.py:171
  (81 shorter events, 25.4 us)
Async XLA Ops:
  7.2 12.4 %copy-start = (bf16[896,512]{1,0:T(8,128)(2,1)S(1)}, bf16[896,512]{1,0:T(8,128)(2,1)}, u32[]{:S(2)}) copy-start(bf16[896,512]{1,0:T(8,128)(2,1)} %param.13) | copy-start | bytes 2752516
  7.2 12.4 %copy-start.14 = (bf16[512,896]{1,0:T(8,128)(2,1)S(1)}, bf16[512,896]{1,0:T(8,128)(2,1)}, u32[]{:S(2)}) copy-start(bf16[512,896]{1,0:T(8,128)(2,1)} %param.11) | copy-start | bytes 2752516
  7.2 39.6 %all-gather.5.cloned.1.call-start = ((), (), s32[]{:S(2)}) async-start(), calls=%async_computation.6 | async-start | bytes 5242880 | tf_op jit(solution)/shard_map/all_gather | solution.py:89
  9.0 122.8 %copy-start.11 = (s32[16]{0:T(128)}, s32[16]{0:T(128)S(1)}, u32[]{:S(2)}) copy-start(s32[16]{0:T(128)S(1)} %multiply_add_fusion) | copy-start | bytes 196
  9.8 13.7 %all-to-all-start = ((s32[8,1,2]{2,1,0:T(1,128)}), s32[8,1,2]{2,1,0:T(1,128)S(1)}, u32[]{:S(2)}, u32[]{:S(2)}) async-start(s32[8,1,2]{2,1,0:T(1,128)} %bitcast), calls=%async_computation | async-start | bytes 8192 | tf_op jit(solution)/shard_map/all_to_all | solution.py:108
  24.8 1.3 copy-start.9
  30.4 6.6 %copy-start.15 = (s32[8]{0:T(128)S(1)}, s32[8]{0:T(128)}, u32[]{:S(2)}) copy-start(s32[8]{0:T(128)} %param.17) | copy-start | bytes 100
  30.4 96.8 %all-to-all-start.1 = ((bf16[8,2,128,1024]{3,2,1,0:T(8,128)(2,1)}), bf16[8,2,128,1024]{3,2,1,0:T(8,128)(2,1)}, u32[]{:S(2)}, u32[]{:S(2)}) async-start(bf16[8,2,128,1024]{3,2,1,0:T(8,128)(2,1)} %bitcast.69), calls=%async_computation.1 | async-start | bytes 8388608 | tf_op jit(solution)/shard_map/all_to_all | solution.py:121
  35.1 47.7 %all-gather.3.cloned.1.call-start = ((), (), s32[]{:S(2)}) async-start(), calls=%async_computation.5 | async-start | bytes 5242880 | tf_op jit(solution)/shard_map/all_gather | solution.py:88
  35.9 291.9 %reduce-scatter.5.cloned.1.call-start = ((), (), s32[]{:S(2)}) async-start(), calls=%async_computation.8 | async-start | bytes 2293760 | tf_op jit(solution)/shard_map/reduce_scatter | solution.py:165
  142.0 1.4 copy-start.1
  142.0 1.4 copy-start.8
  143.4 2.0 copy-start.3
  145.4 7.5 %copy-start.5 = (bf16[8,256,4,128]{3,2,1,0:T(4,128)(2,1)S(1)}, bf16[8,256,4,128]{3,2,1,0:T(4,128)(2,1)}, u32[]{:S(2)}) copy-start(bf16[8,256,4,128]{3,2,1,0:T(4,128)(2,1)} %reshape.200) | copy-start | bytes 6291460
  167.4 1.0 copy-start.6
  176.3 7.7 %copy-start.12 = (s32[16]{0:T(128)S(1)}, s32[16]{0:T(128)}, u32[]{:S(2)}) copy-start(s32[16]{0:T(128)} %copy-done.11) | copy-start | bytes 196
  286.6 2.3 copy-start.10
  292.9 3.1 copy-start.4
  292.9 3.1 copy-start.7
  296.0 3.3 copy-start.2
  299.0 76.4 %reduce-scatter.3.cloned.1.call-start = ((), (), s32[]{:S(2)}) async-start(), calls=%async_computation.7 | async-start | bytes 5242880 | tf_op jit(solution)/shard_map/reduce_scatter | solution.py:171
  299.3 2.5 copy-start.13
Sparse Core Ops, SparseCore 0:
  9.6 37.1 all-gather.4
  48.3 34.4 all-gather.2
  299.1 28.6 reduce-scatter.4
  330.8 44.5 reduce-scatter.2
where the time goes:
time: 388 us; the launch traced here: 382 us
  waiting for transfers between devices  147 us (38%)
  blocking collectives  96.8 us (25%)
  matrix products  52.9 us (14%)
  local copies, waits for them, and re-layouts  47.9 us (12%)
  between operations  14.4 us (4%)
  starting transfers between devices  12.9 us (3%)
  other arithmetic  10 us (3%)
    all_to_all x1, blocking collectives, shards(): lax.all_to_all(returning.reshape(seq_count, slot_cap, RET, 2 * columns),...  96.8 us
    reduce_scatter x1, waiting for transfers between devices, shards(): lax.psum_scatter(lax.optimization_barrier(partial_value.astype(jnp.bfloat...  45.8 us
    all_to_all x1, waiting for transfers between devices, shards(): lax.all_to_all(outgoing.reshape(seq_count, slot_cap, RET, 2 * columns), '...  37.4 us
    all_gather x1, waiting for transfers between devices, shards(): hidden_piece = lax.all_gather(hidden_states, 'head', axis=1, tiled=True)  30.1 us
    unnamed x40, local copies, waits for them, and re-layouts  25.1 us
    reduce_scatter x1, waiting for transfers between devices, shards(): lax.psum_scatter(enc_part, 'head', scatter_dimension=1, tiled=True)  21.6 us
    all_gather x1, waiting for transfers between devices, shards(): grad_piece = lax.all_gather(out_grad, 'head', axis=1, tiled=True)  9.12 us
  transfers between devices with their start and end apart: 6, of which 6 were waited for; matrix products, arithmetic and copies ran while one was open for 9% of the time, Pallas kernels for 0%

commit v1 on v0

--- a/solution.py
+++ b/solution.py
@@ -85,8 +85,13 @@
     highest = lax.Precision.HIGHEST
     contract_last = (((1,), (1,)), ((), ()))
     contract_first = (((0,), (0,)), ((), ()))
-    hidden_piece = lax.all_gather(hidden_states, "head", axis=1, tiled=True)
-    grad_piece = lax.all_gather(out_grad, "head", axis=1, tiled=True)
+    hidden_piece, grad_piece = jnp.split(
+        lax.all_gather(
+            jnp.concatenate([hidden_states, out_grad], axis=0), "head", axis=1, tiled=True
+        ),
+        [hidden_states.shape[0]],
+        axis=0,
+    )
     query_sum = jnp.dot(hidden_piece, w_query, preferred_element_type=jnp.float32)
     grad_sum = lax.dot_general(grad_piece, w_out, contract_last, preferred_element_type=jnp.float32)
     query_sum, grad_sum = (query_sum, grad_sum)

time: 388 us -> 410 us (1.057)
  waiting for transfers between devices: 147 us -> 162 us
  local copies, waits for them, and re-layouts: 47.9 us -> 54.8 us
  other arithmetic: 10 us -> 15.7 us
  matrix products: 52.9 us -> 47.9 us
    all_to_all x1, waiting for transfers between devices: 37.4 us -> 90.3 us  [shards(): lax.all_to_all(outgoing.reshape(seq_count, slot_cap, RET, 2 * columns), '...]
    all_gather x2 -> x1, waiting for transfers between devices: 39.2 us -> 0.02 us  [shards(): lax.all_gather(jnp.concatenate([hidden_states, out_grad], axis=0), 'head'...]
    unnamed x40 -> x48, local copies, waits for them, and re-layouts: 25.1 us -> 25.3 us
  transfers between devices with their start and end apart: 6 -> 5, of which waited for: 6 -> 4; matrix products, arithmetic and copies ran while one was open for 9% -> 9% of each run, Pallas kernels for 0% -> 0%
where the time goes in v1:
time: 410 us; the launch traced here: 404 us
  waiting for transfers between devices  162 us (40%)
  blocking collectives  97 us (24%)
  local copies, waits for them, and re-layouts  54.8 us (13%)
  matrix products  47.9 us (12%)
  other arithmetic  15.7 us (4%)
  between operations  14.6 us (4%)
  starting transfers between devices  12.6 us (3%)
    all_to_all x1, blocking collectives, shards(): lax.all_to_all(returning.reshape(seq_count, slot_cap, RET, 2 * columns),...  97 us
    all_to_all x1, waiting for transfers between devices, shards(): lax.all_to_all(outgoing.reshape(seq_count, slot_cap, RET, 2 * columns), '...  90.3 us
    reduce_scatter x1, waiting for transfers between devices, shards(): lax.psum_scatter(lax.optimization_barrier(partial_value.astype(jnp.bfloat...  46 us
    unnamed x48, local copies, waits for them, and re-layouts  25.3 us
    reduce_scatter x1, waiting for transfers between devices, shards(): lax.psum_scatter(enc_part, 'head', scatter_dimension=1, tiled=True)  21.9 us
  transfers between devices with their start and end apart: 5, of which 4 were waited for; matrix products, arithmetic and copies ran while one was open for 9% of the time, Pallas kernels for 0%

profile of v1, /device:TPU:0, one launch (start us, length us, event | category | flops | bytes accessed | tf_op | source)
XLA Modules:
  0.0 404.3 jit_solution(11221385889116058806)
XLA Ops:
  7.2 3.1 pad_maximum_fusion.1
  12.3 7.3 %all-to-all-start = ((s32[8,1,2]{2,1,0:T(1,128)}), s32[8,1,2]{2,1,0:T(1,128)S(1)}, u32[]{:S(2)}, u32[]{:S(2)}) async-start(s32[8,1,2]{2,1,0:T(1,128)} %bitcast), calls=%async_computation | async-start | bytes 8192 | tf_op jit(solution)/shard_map/all_to_all | solution.py:113
  22.5 3.5 all-to-all-done
  28.6 4.3 %copy.82 = bf16[2,8,128,1024]{3,2,1,0:T(8,128)(2,1)} copy(bf16[2,8,128,1024]{3,1,2,0:T(8,128)(2,1)S(1)} %bitcast.69) | data formatting | bytes 8388608
  32.8 4.7 %all-to-all-start.1 = ((bf16[8,2,128,1024]{3,2,1,0:T(8,128)(2,1)}), bf16[8,2,128,1024]{3,2,1,0:T(8,128)(2,1)}, u32[]{:S(2)}, u32[]{:S(2)}) async-start(bf16[8,2,128,1024]{3,2,1,0:T(8,128)(2,1)} %bitcast.67), calls=%async_computation.1 | async-start | bytes 8388608 | tf_op jit(solution)/shard_map/all_to_all | solution.py:126
  39.3 90.3 %all-to-all-done.1 = bf16[8,2,128,1024]{3,2,1,0:T(8,128)(2,1)} async-done(((bf16[8,2,128,1024]{3,2,1,0:T(8,128)(2,1)}), bf16[8,2,128,1024]{3,2,1,0:T(8,128)(2,1)}, u32[]{:S(2)}, u32[]{:S(2)}) %all-to-all-start.1) | async-done | bytes 4194336 | tf_op jit(solution)/shard_map/all_to_all | solution.py:126
  129.6 4.5 %copy.83 = bf16[2,8,128,1024]{3,1,2,0:T(8,128)(2,1)S(1)} copy(bf16[2,8,128,1024]{3,2,1,0:T(8,128)(2,1)} %bitcast.11) | data formatting | bytes 8388608
  135.4 2.3 copy.84
  137.7 2.6 fusion.69
  140.3 2.5 reshape.199
  142.9 4.5 %reshape.200 = bf16[8,256,4,128]{3,2,1,0:T(4,128)(2,1)} reshape(bf16[16,128,512]{2,1,0:T(8,128)(2,1)} %get-tuple-element.3) | data formatting | bytes 4194304 | tf_op jit(solution)/shard_map/reshape | solution.py:27
  147.4 5.9 %fusion.26 = bf16[512,512]{1,0:T(8,128)(2,1)S(1)} fusion(bf16[4096,512]{1,0:T(8,128)(2,1)} %param.12, bf16[1024,4096]{1,0:T(8,128)(2,1)} %all-gather.2.cloned.1.call-done), kind=kOutput, calls=%fused_computation.30 | convolution fusion | flops 2147745792 | bytes 8912896 | tf_op jit(solution)/shard_map/dot_general | solution.py:95
  154.4 2.4 fusion.29
  162.2 2.0 concatenate.26
  167.0 7.4 %convert_bitcast_fusion = bf16[8,256,4,128]{1,3,2,0:T(8,128)(2,1)} fusion(bf16[8,64,4,128]{3,2,1,0:T(4,128)(2,1)} %concatenate.26, pred[8,64]{1,0:T(8,128)(4,1)} %add_compare_fusion, f32[8,4,64]{2,1,0:T(4,128)S(1)} %get-tuple-element.6, f32[8,4,64,256]{3,2,1,0:T(8,128)} %copy-done.3, pred[8,256]{1,0:T(8,128)(4,1)} %broadcast_bitcast_fusion), kind=kOutput, calls=%fused_computation.12 | convolution fusion | flops 138152192 | bytes 4729344 | tf_op jit(solution)/shard_map/chqk,cqhd->ckhd/dot_general | solution.py:56
  174.4 6.3 %fusion.35 = f32[8,64,4]{1,2,0:T(4,128)} fusion(bf16[8,256,4,128]{3,2,1,0:T(4,128)(2,1)S(1)} %copy-done.5, bf16[8,64,4,128]{3,2,1,0:T(4,128)(2,1)} %concatenate.26, pred[8,64]{1,0:T(8,128)(4,1)} %add_compare_fusion, f32[8,4,64]{2,1,0:T(4,128)S(1)} %get-tuple-element.6, f32[8,4,64,256]{3,2,1,0:T(8,128)} %copy-done.3, pred[8,256]{1,0:T(8,128)(4,1)} %broadcast_bitcast_fusion), kind=kOutput, calls=%fused_computation.35 | convolution fusion | flops 137888000 | bytes 4737536 | tf_op jit(solution)/shard_map/chqk,ckhd->cqhd/dot_general | solution.py:39
  180.7 2.8 copy.74
  183.5 2.4 reshape.191
  185.9 3.3 multiply_convert_fusion.1
  191.4 2.2 reshape.190
  193.6 4.5 %fusion.71 = bf16[2,8,128,1024]{2,1,0,3:T(8,128)(2,1)} fusion(bf16[16,128,512]{1,0,2:T(8,128)(2,1)} %reshape.191, bf16[16,128,512]{1,0,2:T(8,128)(2,1)} %reshape.190), kind=kLoop, calls=%fused_computation.86 | loop fusion | flops 2097152 | bytes 8388608
  198.1 7.4 %copy.86 = bf16[2,8,128,1024]{3,1,2,0:T(8,128)(2,1)} copy(bf16[2,8,128,1024]{2,1,0,3:T(8,128)(2,1)} %fusion.71) | data formatting | bytes 8388608
  205.5 3.5 convolution_convert_fusion
  209.1 2.3 copy.87
  211.4 97.0 %all_to_all.16 = bf16[8,2,128,1024]{3,2,1,0:T(8,128)(2,1)S(1)} all-to-all(bf16[8,2,128,1024]{3,2,1,0:T(8,128)(2,1)S(1)} %bitcast.70), channel_id=1, replica_groups=mesh['seq'=8,'head'=4] {'seq'}, dimensions={0} | all-to-all | bytes 8388608 | tf_op jit(solution)/shard_map/all_to_all | solution.py:150
  308.4 2.3 copy.88
  311.9 2.8 reshape.195
  314.7 3.1 fusion.42
  317.8 3.0 convolution_add_fusion
  323.4 4.3 %convolution_convert_fusion.3 = bf16[512,4096]{1,0:T(8,128)(2,1)} fusion(bf16[4096,512]{1,0:T(8,128)(2,1)S(1)} %copy-done.17, bf16[449,512]{1,0:T(8,128)(2,1)S(1)} %slice.51, bf16[63,512]{1,0:T(8,128)(2,1)S(1)} %slice.50), kind=kOutput, calls=%fused_computation.4 | convolution fusion | flops 2150629376 | bytes 8912896 | tf_op jit(solution)/shard_map/dot_general | solution.py:173
  327.8 21.9 %reduce-scatter.5.cloned.1.call-done = f32[512,224]{0,1:T(8,128)} async-done(((f32[512,896]{0,1:T(8,128)}), f32[512,224]{0,1:T(8,128)}) %reduce-scatter.5.cloned.1.call-update) | async-done | bytes 458768 | tf_op jit(solution)/shard_map/reduce_scatter | solution.py:170
  351.4 46.0 %reduce-scatter.3.cloned.1.call-done = bf16[128,4096]{1,0:T(8,128)(2,1)} async-done(((bf16[512,4096]{1,0:T(8,128)(2,1)}), bf16[128,4096]{1,0:T(8,128)(2,1)}) %reduce-scatter.3.cloned.1.call-update) | async-done | bytes 1048592 | tf_op jit(solution)/shard_map/reduce_scatter | solution.py:176
  (87 shorter events, 27.3 us)
Async XLA Ops:
  7.2 13.2 %copy-start = (bf16[896,512]{1,0:T(8,128)(2,1)S(1)}, bf16[896,512]{1,0:T(8,128)(2,1)}, u32[]{:S(2)}) copy-start(bf16[896,512]{1,0:T(8,128)(2,1)} %param.13) | copy-start | bytes 2752516
  7.2 140.2 %all-gather.2.cloned.1.call-start = ((), (), s32[]{:S(2)}) async-start(), calls=%async_computation.5 | async-start | bytes 10485760 | tf_op jit(solution)/shard_map/all_gather | solution.py:89
  10.3 0.7 copy-start.14
  10.3 9.2 %copy-start.7 = (bf16[896,512]{1,0:T(8,128)(2,1)S(1)}, bf16[896,512]{1,0:T(8,128)(2,1)}, u32[]{:S(2)}) copy-start(bf16[896,512]{1,0:T(8,128)(2,1)} %param.14) | copy-start | bytes 2752516
  10.3 9.2 %copy-start.18 = (bf16[512,896]{1,0:T(8,128)(2,1)S(1)}, bf16[512,896]{1,0:T(8,128)(2,1)}, u32[]{:S(2)}) copy-start(bf16[512,896]{1,0:T(8,128)(2,1)} %param.11) | copy-start | bytes 2752516
  11.4 122.7 %copy-start.12 = (s32[16]{0:T(128)}, s32[16]{0:T(128)S(1)}, u32[]{:S(2)}) copy-start(s32[16]{0:T(128)S(1)} %multiply_add_fusion) | copy-start | bytes 196
  12.3 13.7 %all-to-all-start = ((s32[8,1,2]{2,1,0:T(1,128)}), s32[8,1,2]{2,1,0:T(1,128)S(1)}, u32[]{:S(2)}, u32[]{:S(2)}) async-start(s32[8,1,2]{2,1,0:T(1,128)} %bitcast), calls=%async_computation | async-start | bytes 8192 | tf_op jit(solution)/shard_map/all_to_all | solution.py:113
  27.2 1.3 copy-start.10
  32.8 5.8 %copy-start.19 = (s32[8]{0:T(128)S(1)}, s32[8]{0:T(128)}, u32[]{:S(2)}) copy-start(s32[8]{0:T(128)} %param.17) | copy-start | bytes 100
  32.8 96.8 %all-to-all-start.1 = ((bf16[8,2,128,1024]{3,2,1,0:T(8,128)(2,1)}), bf16[8,2,128,1024]{3,2,1,0:T(8,128)(2,1)}, u32[]{:S(2)}, u32[]{:S(2)}) async-start(bf16[8,2,128,1024]{3,2,1,0:T(8,128)(2,1)} %bitcast.67), calls=%async_computation.1 | async-start | bytes 8388608 | tf_op jit(solution)/shard_map/all_to_all | solution.py:126
  37.6 312.1 %reduce-scatter.5.cloned.1.call-start = ((), (), s32[]{:S(2)}) async-start(), calls=%async_computation.7 | async-start | bytes 2293760 | tf_op jit(solution)/shard_map/reduce_scatter | solution.py:170
  142.9 21.3 %copy-start.1 = (bf16[8,256,4,128]{3,2,1,0:T(4,128)(2,1)}, bf16[8,256,4,128]{3,2,1,0:T(4,128)(2,1)S(1)}, u32[]{:S(2)}) copy-start(bf16[8,256,4,128]{3,2,1,0:T(4,128)(2,1)S(1)} %reshape.199) | copy-start | bytes 6291460
  147.4 6.1 %copy-start.15 = (bf16[1024,4096]{1,0:T(8,128)(2,1)S(1)}, bf16[1024,4096]{1,0:T(8,128)(2,1)}, u32[]{:S(2)}) copy-start(bf16[1024,4096]{1,0:T(8,128)(2,1)} %all-gather.2.cloned.1.call-done) | copy-start | bytes 25165828
  147.4 7.0 %copy-start.16 = (bf16[512,4096]{1,0:T(8,128)(2,1)S(1)}, bf16[512,4096]{1,0:T(8,128)(2,1)}, u32[]{:S(2)}) copy-start(bf16[512,4096]{1,0:T(8,128)(2,1)} %param.15) | copy-start | bytes 12582916
  164.2 0.8 copy-start.9
  165.0 2.0 copy-start.3
  167.0 7.4 %copy-start.5 = (bf16[8,256,4,128]{3,2,1,0:T(4,128)(2,1)S(1)}, bf16[8,256,4,128]{3,2,1,0:T(4,128)(2,1)}, u32[]{:S(2)}) copy-start(bf16[8,256,4,128]{3,2,1,0:T(4,128)(2,1)} %reshape.200) | copy-start | bytes 6291460
  189.2 1.0 copy-start.6
  198.1 7.4 %copy-start.13 = (s32[16]{0:T(128)S(1)}, s32[16]{0:T(128)}, u32[]{:S(2)}) copy-start(s32[16]{0:T(128)} %copy-done.12) | copy-start | bytes 196
  308.4 2.3 copy-start.11
  314.7 3.1 copy-start.4
  314.7 3.1 copy-start.8
  317.8 3.1 copy-start.2
  320.8 76.5 %reduce-scatter.3.cloned.1.call-start = ((), (), s32[]{:S(2)}) async-start(), calls=%async_computation.6 | async-start | bytes 5242880 | tf_op jit(solution)/shard_map/reduce_scatter | solution.py:176
  320.9 2.5 copy-start.17
Sparse Core Ops, SparseCore 0:
  10.5 61.0 all-gather.1
  320.9 28.6 reduce-scatter.4
  352.8 44.5 reduce-scatter.2
